TPU v7x, 32 devices: a whole 2x2x4 slice. The times are simulated.
32 devices in a mesh: img: 8 (over z, y), rep: 4 (over x, core).
Axes of the slice: x: 2, y: 2, z: 4, core: 2. Of those that a mesh axis runs over, the one named last changes fastest.
Arguments:
- descriptors: bfloat16 [16, 256, 1024], P('img', 'rep'), may hold values from -0.5 to 0.5
- cell_counts: int32 [16, 256], P('img', 'rep'), may hold values from 1 to 8
- pair_images: int32 [64, 2], P('img'), may hold values from 0 to 15, as said below
- query_cells: int32 [64, 16], P('img'), may hold values from 0 to 255
- cand_cells: int32 [64, 4, 16], P('img', 'rep'), may hold values from 0 to 255, as said below
- cand_counts: int32 [64, 4], P('img', 'rep'), may hold values from 8 to 16, as said below
Outputs:
- matches: float32 [64, 2, 128], P('img')
- image_score: float32 [16], P('img')
Inputs may be any that keep to these rules, and one draw needn't show every extreme that they name: `pair_images`: the pairs are numbered by blocks of 8: pair k * 8 + j has its first image among images k * 2 to k * 2 + 1 and its second among images j * 2 to j * 2 + 1; the two images of a pair differ. cand_cells[p, r, s] lies in quarter r, between r * 64 and r * 64 + 63; cells may repeat. `cand_counts`: every count is 8 or 16, and every draw holds at least one count of 16.
All inputs are finite; a program needn't handle non-finite values.
Results may differ from a plain program's by a relative error of at most 0.0003.
Values may be sent and summed in bfloat16 or wider, within the bound.
A program may use at most 64 MiB of HBM per device.

v0:
```python
import jax
import jax.numpy as jnp
from jax import lax
from jax.sharding import PartitionSpec as P

DESC = 128
KP = 8
distant = 1000000000.0
group_size = 8


def joined(shard, axis, combine):
    everything = jax.tree.map(lambda part: lax.all_gather(part, axis), shard)
    leading = jax.tree.map(lambda part: part[0], everything)

    def turn(k, so_far):
        return combine(so_far, jax.tree.map(lambda part: part[k], everything))

    return lax.fori_loop(1, lax.axis_size(axis), turn, leading)


def nearest(queries, blocks, block_counts, live_cells):
    pairs = queries.shape[0]
    slots = blocks.shape[1]
    cands = blocks.reshape(pairs, slots * KP, DESC)
    cell_live = jnp.arange(slots, dtype=jnp.int32)[None, :] < live_cells[:, None]
    slot_live = (
        jnp.arange(KP, dtype=jnp.float32)[None, None, :]
        < block_counts.astype(jnp.float32)[:, :, None]
    )
    clive = (cell_live[:, :, None] & slot_live).reshape(pairs, slots * KP)
    groups = pairs // group_size

    def one_group(packed):
        query_part, cand_part, live_part = packed
        qwide = query_part.astype(jnp.float32)
        cwide = cand_part.astype(jnp.float32)
        qnorm = jnp.sum(qwide * qwide, axis=2)
        cnorm = jnp.sum(cwide * cwide, axis=2)
        inner = jnp.einsum(
            "pqd,pcd->pqc", query_part, cand_part, preferred_element_type=jnp.float32
        )
        dist = qnorm[:, :, None] + cnorm[:, None, :] - 2.0 * inner
        dist = jnp.where(live_part[:, None, :], dist, jnp.float32(distant))
        lowest = -lax.top_k(-dist, 2)[0]
        return (lowest[..., 0], lowest[..., 1])

    packed = (
        queries.reshape(groups, group_size, -1, DESC),
        cands.reshape(groups, group_size, -1, DESC),
        clive.reshape(groups, group_size, -1),
    )
    best, runner = lax.map(one_group, packed)
    return (best.reshape(pairs, -1), runner.reshape(pairs, -1))


def keep_two(left, right):
    low = jnp.minimum(left[0], right[0])
    high = jnp.minimum(jnp.maximum(left[0], right[0]), jnp.minimum(left[1], right[1]))
    return (low, high)


def on_device(descriptors, cell_counts, pair_images, query_cells, cand_cells, cand_counts):
    img_dev, share, width = descriptors.shape
    peers = lax.axis_size("img")
    whole, whole_counts = (
        lax.all_gather(descriptors, "rep", axis=1, tiled=True),
        lax.all_gather(cell_counts.astype(jnp.bfloat16), "rep", axis=1, tiled=True),
    )
    cells = whole.shape[1]
    first_local = pair_images[:, 0] % img_dev
    second_local = pair_images[:, 1] % img_dev
    query_rows = (first_local[:, None] * cells + query_cells).reshape(-1)
    queries = jnp.take(whole.reshape(img_dev * cells, width), query_rows, axis=0).reshape(
        peers, -1, DESC
    )
    query_counts = jnp.take(whole_counts.reshape(img_dev * cells), query_rows).reshape(peers, -1)
    qlive = (
        jnp.arange(KP, dtype=jnp.float32)[None, None, :]
        < query_counts.astype(jnp.float32)[:, :, None]
    ).reshape(peers, -1)
    lists = cand_cells[:, 0, :]
    live_cells = cand_counts[:, 0]
    local_rows = descriptors.reshape(img_dev * share, width)
    local_counts = cell_counts.reshape(img_dev * share)
    asked, asked_image = (
        lax.all_to_all(lists, "img", split_axis=0, concat_axis=0, tiled=True),
        lax.all_to_all(second_local, "img", split_axis=0, concat_axis=0, tiled=True),
    )
    rows = (asked_image[:, None] * share + asked % share).reshape(-1)
    blocks = jnp.take(local_rows, rows, axis=0).reshape(peers, -1, width)
    block_counts = jnp.take(local_counts, rows).reshape(peers, -1).astype(jnp.bfloat16)
    blocks, block_counts = (
        lax.all_to_all(blocks, "img", split_axis=0, concat_axis=0, tiled=True),
        lax.all_to_all(block_counts, "img", split_axis=0, concat_axis=0, tiled=True),
    )
    best, runner = nearest(queries, blocks, block_counts, live_cells)
    best, runner = joined((best, runner), "rep", keep_two)
    best = jnp.where(qlive, best, jnp.float32(0.0))
    runner = jnp.where(qlive, runner, jnp.float32(0.0))
    matches = jnp.stack([best, runner], axis=1)
    margin = jnp.where(qlive, (runner - best) / (runner + 1.0), jnp.float32(0.0))
    score = jnp.sum(margin, axis=1) / jnp.sum(qlive.astype(jnp.float32), axis=1)
    arrived = lax.all_to_all(score, "img", split_axis=0, concat_axis=0, tiled=True)
    image_ids = jnp.arange(img_dev, dtype=jnp.int32)
    own_part = jnp.sum(
        jnp.where(first_local[:, None] == image_ids[None, :], score[:, None], jnp.float32(0.0)),
        axis=0,
    )
    other_part = jnp.sum(
        jnp.where(asked_image[:, None] == image_ids[None, :], arrived[:, None], jnp.float32(0.0)),
        axis=0,
    )
    return (matches, own_part + other_part)


def solution(mesh):
    in_specs = (
        P("img", "rep", None),
        P("img", "rep"),
        P("img", None),
        P("img", None),
        P("img", "rep", None),
        P("img", "rep"),
    )
    out_specs = (P("img", None, None), P("img"))
    return jax.shard_map(
        on_device, mesh=mesh, in_specs=in_specs, out_specs=out_specs, check_vma=False
    )
```

profile of v0, /device:TPU:0, one launch (start us, length us, event | category | flops | bytes accessed | tf_op | source)
XLA Modules:
  0.0 107.9 jit_solution(14698842884387432103)
XLA Ops:
  7.2 0.7 all-gather.5.cloned.1.call-update
  7.9 0.7 copy.43
  8.6 7.3 %all-to-all-start = ((s32[8,1,1]{2,1,0:T(1,128)}), s32[8,1,1]{2,1,0:T(1,128)S(1)}, u32[]{:S(2)}, u32[]{:S(2)}) async-start(s32[8,1,1]{2,1,0:T(1,128)} %copy.43), calls=%async_computation | async-start | bytes 8192 | tf_op jit(solution)/shard_map/all_to_all | solution.py:88
  15.9 0.7 copy-done.3
  16.6 0.7 copy-done.4
  17.3 5.0 %all-gather.2 = bf16[4,64,2]{1,2,0:T(2,128)(2,1)S(1)} all-gather(bf16[1,64,2]{1,2,0:T(2,128)(2,1)S(1)} %convert_bitcast_fusion), channel_id=1, replica_groups=mesh['img'=8,'rep'=4] {'rep'}, dimensions={0}, use_global_device_ids=true | all-gather | bytes 1280 | tf_op jit(solution)/shard_map/all_gather | solution.py:68
  22.5 0.6 copy-done.1
  23.2 1.3 %gather_fusion = bf16[128]{0:T(256)(128)(2,1)S(1)} fusion(bf16[512]{0:T(512)(128)(2,1)S(1)} %bitcast.56, s32[1024]{0:T(1024)S(1)} %pad_clamp_fusion.1), kind=kCustom, calls=%fused_computation | custom fusion | bytes 1024 | tf_op jit(solution)/shard_map/jit(_take)/gather | solution.py:77
  24.8 6.0 %all-to-all-start.1 = ((s32[8,1,16]{2,1,0:T(1,128)}), s32[8,1,16]{2,1,0:T(1,128)S(1)}, u32[]{:S(2)}, u32[]{:S(2)}) async-start(s32[8,1,16]{2,1,0:T(1,128)} %param.12), calls=%async_computation.1 | async-start | bytes 8192 | tf_op jit(solution)/shard_map/all_to_all | solution.py:87
  30.8 0.2 reduce.1
  31.2 6.0 %all-to-all-done.1 = s32[8,1,16]{2,1,0:T(1,128)S(1)} async-done(((s32[8,1,16]{2,1,0:T(1,128)}), s32[8,1,16]{2,1,0:T(1,128)S(1)}, u32[]{:S(2)}, u32[]{:S(2)}) %all-to-all-start.1) | async-done | bytes 544 | tf_op jit(solution)/shard_map/all_to_all | solution.py:87
  37.2 0.5 broadcast.286
  37.7 0.7 reduce.6
  38.5 1.2 %gather_fusion.1 = s32[128]{0:T(128)S(1)} fusion(s32[128]{0:T(128)S(1)} %reshape.315, s32[1024]{0:T(1024)S(1)} %pad_clamp_fusion), kind=kCustom, calls=%fused_computation.1 | custom fusion | bytes 1536 | tf_op jit(solution)/shard_map/jit(_take)/gather | solution.py:92
  39.9 0.6 copy.47
  40.5 3.3 %all-to-all-start.2 = ((bf16[8,1,16]{2,1,0:T(2,128)(2,1)}), bf16[8,1,16]{2,1,0:T(2,128)(2,1)S(1)}, u32[]{:S(2)}, u32[]{:S(2)}) async-start(bf16[8,1,16]{2,1,0:T(2,128)(2,1)} %copy.47), calls=%async_computation.2 | async-start | bytes 8192 | tf_op jit(solution)/shard_map/all_to_all | solution.py:95
  43.8 0.9 gather_fusion.3
  44.7 0.8 broadcast_select_fusion
  45.6 4.6 %all-to-all-done.2 = bf16[8,1,16]{2,1,0:T(2,128)(2,1)S(1)} async-done(((bf16[8,1,16]{2,1,0:T(2,128)(2,1)}), bf16[8,1,16]{2,1,0:T(2,128)(2,1)S(1)}, u32[]{:S(2)}, u32[]{:S(2)}) %all-to-all-start.2) | async-done | bytes 288 | tf_op jit(solution)/shard_map/all_to_all | solution.py:95
  50.1 3.4 %all-to-all-start.3 = ((bf16[8,16,1024]{2,1,0:T(8,128)(2,1)}), bf16[8,16,1024]{2,1,0:T(8,128)(2,1)S(1)}, u32[]{:S(2)}, u32[]{:S(2)}) async-start(bf16[8,16,1024]{2,1,0:T(8,128)(2,1)} %broadcast_select_fusion), calls=%async_computation.3 | async-start | bytes 524288 | tf_op jit(solution)/shard_map/all_to_all | solution.py:94
  54.6 7.1 %all-to-all-done.3 = bf16[8,16,1024]{2,1,0:T(8,128)(2,1)S(1)} async-done(((bf16[8,16,1024]{2,1,0:T(8,128)(2,1)}), bf16[8,16,1024]{2,1,0:T(8,128)(2,1)S(1)}, u32[]{:S(2)}, u32[]{:S(2)}) %all-to-all-start.3) | async-done | bytes 262176 | tf_op jit(solution)/shard_map/all_to_all | solution.py:94
  62.1 2.4 %gather_fusion.2 = bf16[128,1024]{1,0:T(8,128)(2,1)S(1)} fusion(bf16[512,1024]{1,0:T(8,128)(2,1)} %bitcast.58, s32[1024]{0:T(1024)S(1)} %pad_clamp_fusion.1), kind=kCustom, calls=%fused_computation.2 | custom fusion | bytes 524800 | tf_op jit(solution)/shard_map/jit(_take)/gather | solution.py:74
  64.6 0.3 convolution_multiply_fusion
  64.9 2.6 %fusion.5 = f32[8,128,128]{2,1,0:T(8,128)S(1)} fusion(f32[8,128,128]{2,1,0:T(8,128)S(1)} %convolution_multiply_fusion, f32[8,128]{1,0:T(8,128)S(1)} %multiply_reduce_fusion, pred[8,128]{1,0:T(8,128)(4,1)S(1)} %compare_and_fusion.1, bf16[8,128,128]{2,1,0:T(8,128)(2,1)S(1)} %gather.29, pred[8,128]{1,0:T(8,128)(4,1)S(1)} %broadcast_in_dim.111), kind=kOutput, calls=%fused_computation.12 | output fusion | flops 918655 | bytes 1316864 | tf_op jit(solution)/shard_map/while/body/eval_jaxpr/add | solution.py:43
  67.8 10.5 %top_k.9 = (f32[8,128,128]{1,2,0:T(8,128)S(1)}, s32[8,128,128]{1,2,0:T(8,128)}) sort(f32[8,128,128]{1,2,0:T(8,128)S(1)} %copy.55, s32[8,128,128]{1,2,0:T(8,128)S(1)} %iota.21.clone), dimensions={2}, to_apply=%region_2.3 | sort | flops 2228224 | bytes 2097152 | tf_op jit(solution)/shard_map/while/body/eval_jaxpr/top_k | solution.py:45
  79.1 5.2 %all-gather = f32[32,128,1]{1,2,0:T(1,128)S(1)} all-gather(f32[8,128,1]{1,2,0:T(1,128)S(1)} %copy.49), channel_id=2, replica_groups=mesh['img'=8,'rep'=4] {'rep'}, dimensions={0}, use_global_device_ids=true | all-gather | bytes 20480 | tf_op jit(solution)/shard_map/all_gather | solution.py:13
  84.3 5.2 %all-gather.1 = f32[32,128,1]{1,2,0:T(1,128)S(1)} all-gather(f32[8,128,1]{1,2,0:T(1,128)S(1)} %copy.51), channel_id=3, replica_groups=mesh['img'=8,'rep'=4] {'rep'}, dimensions={0}, use_global_device_ids=true | all-gather | bytes 20480 | tf_op jit(solution)/shard_map/all_gather | solution.py:13
  89.8 0.7 copy.53
  90.5 3.3 %all-to-all-start.4 = ((f32[8,1,1]{2,1,0:T(1,128)}), f32[8,1,1]{2,1,0:T(1,128)S(1)}, u32[]{:S(2)}, u32[]{:S(2)}) async-start(f32[8,1,1]{2,1,0:T(1,128)} %copy.53), calls=%async_computation.4 | async-start | bytes 8192 | tf_op jit(solution)/shard_map/all_to_all | solution.py:104
  93.8 0.6 copy.54
  94.4 5.8 %all-to-all-done.4 = f32[8,1,1]{2,1,0:T(1,128)S(1)} async-done(((f32[8,1,1]{2,1,0:T(1,128)}), f32[8,1,1]{2,1,0:T(1,128)S(1)}, u32[]{:S(2)}, u32[]{:S(2)}) %all-to-all-start.4) | async-done | bytes 64 | tf_op jit(solution)/shard_map/all_to_all | solution.py:104
  100.5 0.5 add.234
  (69 shorter events, 4.3 us)
Async XLA Ops:
  7.2 0.7 copy-start.2
  7.2 54.9 %all-gather.5.cloned.1.call-start = ((), (), s32[]{:S(2)}) async-start(), calls=%async_computation.5 | async-start | bytes 1310720 | tf_op jit(solution)/shard_map/all_gather | solution.py:67
  8.6 16.1 %all-to-all-start = ((s32[8,1,1]{2,1,0:T(1,128)}), s32[8,1,1]{2,1,0:T(1,128)S(1)}, u32[]{:S(2)}, u32[]{:S(2)}) async-start(s32[8,1,1]{2,1,0:T(1,128)} %copy.43), calls=%async_computation | async-start | bytes 8192 | tf_op jit(solution)/shard_map/all_to_all | solution.py:88
  15.9 0.7 copy-start.3
  16.6 0.7 copy-start.4
  22.4 0.7 copy-start.1
  24.8 12.4 %all-to-all-start.1 = ((s32[8,1,16]{2,1,0:T(1,128)}), s32[8,1,16]{2,1,0:T(1,128)S(1)}, u32[]{:S(2)}, u32[]{:S(2)}) async-start(s32[8,1,16]{2,1,0:T(1,128)} %param.12), calls=%async_computation.1 | async-start | bytes 8192 | tf_op jit(solution)/shard_map/all_to_all | solution.py:87
  38.5 5.3 %copy-start = (bf16[2,64,1024]{2,1,0:T(8,128)(2,1)S(1)}, bf16[2,64,1024]{2,1,0:T(8,128)(2,1)}, u32[]{:S(2)}) copy-start(bf16[2,64,1024]{2,1,0:T(8,128)(2,1)} %param.8) | copy-start | bytes 786436
  40.5 9.7 %all-to-all-start.2 = ((bf16[8,1,16]{2,1,0:T(2,128)(2,1)}), bf16[8,1,16]{2,1,0:T(2,128)(2,1)S(1)}, u32[]{:S(2)}, u32[]{:S(2)}) async-start(bf16[8,1,16]{2,1,0:T(2,128)(2,1)} %copy.47), calls=%async_computation.2 | async-start | bytes 8192 | tf_op jit(solution)/shard_map/all_to_all | solution.py:95
  50.1 11.6 %all-to-all-start.3 = ((bf16[8,16,1024]{2,1,0:T(8,128)(2,1)}), bf16[8,16,1024]{2,1,0:T(8,128)(2,1)S(1)}, u32[]{:S(2)}, u32[]{:S(2)}) async-start(bf16[8,16,1024]{2,1,0:T(8,128)(2,1)} %broadcast_select_fusion), calls=%async_computation.3 | async-start | bytes 524288 | tf_op jit(solution)/shard_map/all_to_all | solution.py:94
  90.5 9.8 %all-to-all-start.4 = ((f32[8,1,1]{2,1,0:T(1,128)}), f32[8,1,1]{2,1,0:T(1,128)S(1)}, u32[]{:S(2)}, u32[]{:S(2)}) async-start(f32[8,1,1]{2,1,0:T(1,128)} %copy.53), calls=%async_computation.4 | async-start | bytes 8192 | tf_op jit(solution)/shard_map/all_to_all | solution.py:104
Sparse Core Ops, SparseCore 0:
  9.5 19.4 all-gather.4
where the time goes:
time: 108 us
  waiting for transfers between devices  24.2 us (22%)
  starting transfers between devices  23.4 us (22%)
  other arithmetic  16.7 us (15%)
  blocking collectives  15.4 us (14%)
  between operations  14.3 us (13%)
  local copies, waits for them, and re-layouts  13.5 us (12%)
    top_k x1, other arithmetic, one_group(): lowest = -lax.top_k(-dist, 2)[0]  10.5 us
    all_gather x2, blocking collectives, joined(): everything = jax.tree.map(lambda part: lax.all_gather(part, axis), shard)  10.4 us
    all_to_all x1, starting transfers between devices, on_device(): lax.all_to_all(second_local, 'img', split_axis=0, concat_axis=0, tiled=True)  7.31 us
    all_to_all x1, waiting for transfers between devices, on_device(): lax.all_to_all(blocks, 'img', split_axis=0, concat_axis=0, tiled=True)  7.07 us
    all_to_all x1, waiting for transfers between devices, on_device(): lax.all_to_all(lists, 'img', split_axis=0, concat_axis=0, tiled=True)  6.02 us
    all_to_all x1, starting transfers between devices, on_device(): lax.all_to_all(lists, 'img', split_axis=0, concat_axis=0, tiled=True)  6.01 us
    all_to_all x1, waiting for transfers between devices, on_device(): lax.all_to_all(score, 'img', split_axis=0, concat_axis=0, tiled=True)  5.81 us
    all_gather x1, blocking collectives, on_device(): lax.all_gather(cell_counts.astype(jnp.bfloat16), 'rep', axis=1, tiled=True)  5.05 us
  transfers between devices with their start and end apart: 6, of which 4 were waited for; matrix products, arithmetic and copies ran while one was open for 9% of the time, Pallas kernels for 0%

commit v1 on v0

--- a/solution.py
+++ b/solution.py
@@ -1,3 +1,4 @@
+import functools
 import jax
 import jax.numpy as jnp
 from jax import lax
@@ -7,6 +8,43 @@
 KP = 8
 distant = 1000000000.0
 group_size = 8
+
+
+def _resolve_leaves(array_in, d0, mine_x):
+    before, prior = (array_in.shape[:d0], array_in.shape[d0 + 1 :])
+    return jnp.moveaxis(array_in.reshape(*before, mine_x, -1, *prior), d0, 0)
+
+
+def perform_region_in(inp, dimension_no):
+    inp = jnp.moveaxis(inp, 0, dimension_no)
+    front = inp.shape
+    return inp.reshape(
+        *front[:dimension_no],
+        front[dimension_no] * front[dimension_no + 1],
+        *front[dimension_no + 2 :]
+    )
+
+
+def review_the_frame(v0, a_name, block_in, vec):
+    far_arr, block_next = (lax.psum(1, a_name), lax.axis_index(a_name))
+    z1 = _resolve_leaves(v0, block_in, far_arr)
+    all_rows = [z1[block_next]]
+    dev_i = 1
+    while dev_i < far_arr:
+        local_part = z1[(block_next + dev_i) % far_arr]
+        all_rows.append(
+            lax.ppermute(
+                local_part,
+                axis_name=a_name,
+                perm=[(j, (j + dev_i) % far_arr) for j in range(far_arr)],
+            )
+        )
+        dev_i = dev_i + 1
+    z1 = jnp.stack(all_rows)[(block_next - jnp.arange(far_arr)) % far_arr]
+    return perform_region_in(z1, vec)
+
+
+solve_wall = functools.partial(review_the_frame, a_name="img", block_in=0, vec=0)
 
 
 def joined(shard, axis, combine):
@@ -92,7 +130,7 @@
     block_counts = jnp.take(local_counts, rows).reshape(peers, -1).astype(jnp.bfloat16)
     blocks, block_counts = (
         lax.all_to_all(blocks, "img", split_axis=0, concat_axis=0, tiled=True),
-        lax.all_to_all(block_counts, "img", split_axis=0, concat_axis=0, tiled=True),
+        solve_wall(block_counts),
     )
     best, runner = nearest(queries, blocks, block_counts, live_cells)
     best, runner = joined((best, runner), "rep", keep_two)

time: 108 us -> 115 us (1.065)
  starting transfers between devices: 23.4 us -> 30 us
    ppermute x0 -> x7, waiting for transfers between devices: none -> 11 us  [review_the_frame(): lax.ppermute(local_part, axis_name=a_name, perm=[(j, (j + dev_i) % far_ar...]
    ppermute x0 -> x7, starting transfers between devices: none -> 7.6 us  [review_the_frame(): lax.ppermute(local_part, axis_name=a_name, perm=[(j, (j + dev_i) % far_ar...]
    all_to_all x1, waiting for transfers between devices: 7.07 us -> 0.01 us  [on_device(): lax.all_to_all(blocks, 'img', split_axis=0, concat_axis=0, tiled=True)]
    all_to_all x1 -> x0, waiting for transfers between devices: 4.59 us -> none  [on_device(): lax.all_to_all(block_counts, 'img', split_axis=0, concat_axis=0, tiled=True)]
    all_to_all x1 -> x0, starting transfers between devices: 3.31 us -> none  [on_device(): lax.all_to_all(block_counts, 'img', split_axis=0, concat_axis=0, tiled=True)]
    all_to_all x1, starting transfers between devices: 3.41 us -> 5.42 us  [on_device(): lax.all_to_all(blocks, 'img', split_axis=0, concat_axis=0, tiled=True)]
    unnamed x14 -> x22, local copies, waits for them, and re-layouts: 2.81 us -> 2.96 us
  transfers between devices with their start and end apart: 6 -> 12, of which waited for: 4 -> 4; matrix products, arithmetic and copies ran while one was open for 9% -> 9% of each run, Pallas kernels for 0% -> 0%
where the time goes in v1:
time: 115 us; the launch traced here: 114 us
  starting transfers between devices  30 us (26%)
  waiting for transfers between devices  23.6 us (21%)
  other arithmetic  16.7 us (15%)
  blocking collectives  15.4 us (13%)
  between operations  14.4 us (13%)
  local copies, waits for them, and re-layouts  13.6 us (12%)
    ppermute x7, waiting for transfers between devices, review_the_frame(): lax.ppermute(local_part, axis_name=a_name, perm=[(j, (j + dev_i) % far_ar...  11 us
    top_k x1, other arithmetic, one_group(): lowest = -lax.top_k(-dist, 2)[0]  10.5 us
    all_gather x2, blocking collectives, joined(): everything = jax.tree.map(lambda part: lax.all_gather(part, axis), shard)  10.4 us
    ppermute x7, starting transfers between devices, review_the_frame(): lax.ppermute(local_part, axis_name=a_name, perm=[(j, (j + dev_i) % far_ar...  7.6 us
    all_to_all x1, starting transfers between devices, on_device(): lax.all_to_all(second_local, 'img', split_axis=0, concat_axis=0, tiled=True)  7.31 us
    all_to_all x1, waiting for transfers between devices, on_device(): lax.all_to_all(lists, 'img', split_axis=0, concat_axis=0, tiled=True)  6.02 us
    all_to_all x1, starting transfers between devices, on_device(): lax.all_to_all(lists, 'img', split_axis=0, concat_axis=0, tiled=True)  6.01 us
    all_to_all x1, waiting for transfers between devices, on_device(): lax.all_to_all(score, 'img', split_axis=0, concat_axis=0, tiled=True)  5.88 us
  transfers between devices with their start and end apart: 12, of which 4 were waited for; matrix products, arithmetic and copies ran while one was open for 9% of the time, Pallas kernels for 0%

profile of v1, /device:TPU:0, one launch (start us, length us, event | category | flops | bytes accessed | tf_op | source)
XLA Modules:
  0.0 114.1 jit_solution(15830332560504911571)
XLA Ops:
  7.2 0.7 all-gather.5.cloned.1.call-update
  7.9 0.7 copy.33
  8.6 7.3 %all-to-all-start = ((s32[8,1,1]{2,1,0:T(1,128)}), s32[8,1,1]{2,1,0:T(1,128)S(1)}, u32[]{:S(2)}, u32[]{:S(2)}) async-start(s32[8,1,1]{2,1,0:T(1,128)} %copy.33), calls=%async_computation | async-start | bytes 8192 | tf_op jit(solution)/shard_map/all_to_all | solution.py:126
  15.9 0.7 copy-done.2
  16.7 0.6 copy-done.4
  17.4 5.0 %all-gather.2 = bf16[4,64,2]{1,2,0:T(2,128)(2,1)S(1)} all-gather(bf16[1,64,2]{1,2,0:T(2,128)(2,1)S(1)} %convert_bitcast_fusion), channel_id=1, replica_groups=mesh['img'=8,'rep'=4] {'rep'}, dimensions={0}, use_global_device_ids=true | all-gather | bytes 1280 | tf_op jit(solution)/shard_map/all_gather | solution.py:106
  22.6 0.7 copy-done.1
  23.4 1.3 %gather_fusion = bf16[128]{0:T(256)(128)(2,1)S(1)} fusion(bf16[512]{0:T(512)(128)(2,1)S(1)} %bitcast.73, s32[1024]{0:T(1024)S(1)} %pad_clamp_fusion.2), kind=kCustom, calls=%fused_computation | custom fusion | bytes 1024 | tf_op jit(solution)/shard_map/jit(_take)/gather | solution.py:115
  25.8 6.0 %all-to-all-start.1 = ((s32[8,1,16]{2,1,0:T(1,128)}), s32[8,1,16]{2,1,0:T(1,128)S(1)}, u32[]{:S(2)}, u32[]{:S(2)}) async-start(s32[8,1,16]{2,1,0:T(1,128)} %param.12), calls=%async_computation.1 | async-start | bytes 8192 | tf_op jit(solution)/shard_map/all_to_all | solution.py:125
  32.2 6.0 %all-to-all-done.1 = s32[8,1,16]{2,1,0:T(1,128)S(1)} async-done(((s32[8,1,16]{2,1,0:T(1,128)}), s32[8,1,16]{2,1,0:T(1,128)S(1)}, u32[]{:S(2)}, u32[]{:S(2)}) %all-to-all-start.1) | async-done | bytes 544 | tf_op jit(solution)/shard_map/all_to_all | solution.py:125
  38.7 0.7 reduce.6
  39.5 1.2 %gather_fusion.1 = s32[128]{0:T(128)S(1)} fusion(s32[128]{0:T(128)S(1)} %reshape.372, s32[1024]{0:T(1024)S(1)} %pad_clamp_fusion.1), kind=kCustom, calls=%fused_computation.1 | custom fusion | bytes 1536 | tf_op jit(solution)/shard_map/jit(_take)/gather | solution.py:130
  40.9 0.6 collective-permute-start.6
  41.6 1.4 %collective-permute-start.5 = (bf16[1,16]{1,0:T(2,128)(2,1)S(1)}, bf16[1,16]{1,0:T(2,128)(2,1)S(1)}, u32[]{:S(2)}, u32[]{:S(2)}) collective-permute-start(bf16[1,16]{1,0:T(2,128)(2,1)S(1)} %get-tuple-element.193), channel_id=1, source_target_pairs={{0,24},{4,28},{8,0},{12,4},{16,8},{20,12},{24,16},{28,20},{1,25},{... | collective-permute-start | bytes 104 | tf_op jit(solution)/shard_map/ppermute | solution.py:36
  43.0 1.5 %collective-permute-start.4 = (bf16[1,16]{1,0:T(2,128)(2,1)S(1)}, bf16[1,16]{1,0:T(2,128)(2,1)S(1)}, u32[]{:S(2)}, u32[]{:S(2)}) collective-permute-start(bf16[1,16]{1,0:T(2,128)(2,1)S(1)} %get-tuple-element.194), channel_id=1, source_target_pairs={{0,20},{4,24},{8,28},{12,0},{16,4},{20,8},{24,12},{28,16},{1,21},{... | collective-permute-start | bytes 104 | tf_op jit(solution)/shard_map/ppermute | solution.py:36
  44.5 1.5 %collective-permute-start.3 = (bf16[1,16]{1,0:T(2,128)(2,1)S(1)}, bf16[1,16]{1,0:T(2,128)(2,1)S(1)}, u32[]{:S(2)}, u32[]{:S(2)}) collective-permute-start(bf16[1,16]{1,0:T(2,128)(2,1)S(1)} %get-tuple-element.195), channel_id=1, source_target_pairs={{0,16},{4,20},{8,24},{12,28},{16,0},{20,4},{24,8},{28,12},{1,17},{... | collective-permute-start | bytes 104 | tf_op jit(solution)/shard_map/ppermute | solution.py:36
  46.0 0.6 collective-permute-start
  46.5 0.9 gather_fusion.4
  47.4 0.8 broadcast_select_fusion
  48.2 5.4 %all-to-all-start.2 = ((bf16[8,16,1024]{2,1,0:T(8,128)(2,1)}), bf16[8,16,1024]{2,1,0:T(8,128)(2,1)S(1)}, u32[]{:S(2)}, u32[]{:S(2)}) async-start(bf16[8,16,1024]{2,1,0:T(8,128)(2,1)} %broadcast_select_fusion), calls=%async_computation.2 | async-start | bytes 524288 | tf_op jit(solution)/shard_map/all_to_all | solution.py:132
  53.6 2.0 %collective-permute-start.1 = (bf16[1,16]{1,0:T(2,128)(2,1)S(1)}, bf16[1,16]{1,0:T(2,128)(2,1)S(1)}, u32[]{:S(2)}, u32[]{:S(2)}) collective-permute-start(bf16[1,16]{1,0:T(2,128)(2,1)S(1)} %get-tuple-element.197), channel_id=1, source_target_pairs={{0,8},{4,12},{8,16},{12,20},{16,24},{20,28},{24,0},{28,4},{1,9},{5... | collective-permute-start | bytes 104 | tf_op jit(solution)/shard_map/ppermute | solution.py:36
  55.7 5.6 %collective-permute-done.1 = bf16[1,16]{1,0:T(2,128)(2,1)S(1)} collective-permute-done((bf16[1,16]{1,0:T(2,128)(2,1)S(1)}, bf16[1,16]{1,0:T(2,128)(2,1)S(1)}, u32[]{:S(2)}, u32[]{:S(2)}) %collective-permute-start.1) | collective-permute-done | bytes 64 | tf_op jit(solution)/shard_map/ppermute | solution.py:36
  61.3 5.4 %collective-permute-done.2 = bf16[1,16]{1,0:T(2,128)(2,1)S(1)} collective-permute-done((bf16[1,16]{1,0:T(2,128)(2,1)S(1)}, bf16[1,16]{1,0:T(2,128)(2,1)S(1)}, u32[]{:S(2)}, u32[]{:S(2)}) %collective-permute-start.2) | collective-permute-done | bytes 64 | tf_op jit(solution)/shard_map/ppermute | solution.py:36
  67.9 2.4 %gather_fusion.3 = bf16[128,1024]{1,0:T(8,128)(2,1)S(1)} fusion(bf16[512,1024]{1,0:T(8,128)(2,1)} %bitcast.75, s32[1024]{0:T(1024)S(1)} %pad_clamp_fusion.2), kind=kCustom, calls=%fused_computation.3 | custom fusion | bytes 524800 | tf_op jit(solution)/shard_map/jit(_take)/gather | solution.py:112
  70.8 2.6 %fusion.5 = f32[8,128,128]{2,1,0:T(8,128)S(1)} fusion(f32[8,128,128]{2,1,0:T(8,128)S(1)} %convolution_multiply_fusion, f32[8,128]{1,0:T(8,128)S(1)} %multiply_reduce_fusion, pred[8,128]{1,0:T(8,128)(4,1)S(1)} %compare_and_fusion, bf16[8,128,128]{2,1,0:T(8,128)(2,1)S(1)} %gather.33, pred[8,128]{1,0:T(8,128)(4,1)S(1)} %broadcast_in_dim.112), kind=kOutput, calls=%fused_computation.13 | output fusion | flops 918655 | bytes 1316864 | tf_op jit(solution)/shard_map/while/body/eval_jaxpr/add | solution.py:81
  73.6 10.5 %top_k.9 = (f32[8,128,128]{1,2,0:T(8,128)S(1)}, s32[8,128,128]{1,2,0:T(8,128)}) sort(f32[8,128,128]{1,2,0:T(8,128)S(1)} %copy.40, s32[8,128,128]{1,2,0:T(8,128)S(1)} %iota.26.clone), dimensions={2}, to_apply=%region_2.3 | sort | flops 2228224 | bytes 2097152 | tf_op jit(solution)/shard_map/while/body/eval_jaxpr/top_k | solution.py:83
  84.9 5.2 %all-gather = f32[32,128,1]{1,2,0:T(1,128)S(1)} all-gather(f32[8,128,1]{1,2,0:T(1,128)S(1)} %copy.34), channel_id=2, replica_groups=mesh['img'=8,'rep'=4] {'rep'}, dimensions={0}, use_global_device_ids=true | all-gather | bytes 20480 | tf_op jit(solution)/shard_map/all_gather | solution.py:51
  90.1 5.2 %all-gather.1 = f32[32,128,1]{1,2,0:T(1,128)S(1)} all-gather(f32[8,128,1]{1,2,0:T(1,128)S(1)} %copy.36), channel_id=3, replica_groups=mesh['img'=8,'rep'=4] {'rep'}, dimensions={0}, use_global_device_ids=true | all-gather | bytes 20480 | tf_op jit(solution)/shard_map/all_gather | solution.py:51
  95.6 0.7 copy.38
  96.3 3.6 %all-to-all-start.3 = ((f32[8,1,1]{2,1,0:T(1,128)}), f32[8,1,1]{2,1,0:T(1,128)S(1)}, u32[]{:S(2)}, u32[]{:S(2)}) async-start(f32[8,1,1]{2,1,0:T(1,128)} %copy.38), calls=%async_computation.3 | async-start | bytes 8192 | tf_op jit(solution)/shard_map/all_to_all | solution.py:142
  100.0 0.6 copy.39
  100.6 5.9 %all-to-all-done.3 = f32[8,1,1]{2,1,0:T(1,128)S(1)} async-done(((f32[8,1,1]{2,1,0:T(1,128)}), f32[8,1,1]{2,1,0:T(1,128)S(1)}, u32[]{:S(2)}, u32[]{:S(2)}) %all-to-all-start.3) | async-done | bytes 64 | tf_op jit(solution)/shard_map/all_to_all | solution.py:142
  (91 shorter events, 6.5 us)
Async XLA Ops:
  7.2 0.7 copy-start.3
  7.2 60.7 %all-gather.5.cloned.1.call-start = ((), (), s32[]{:S(2)}) async-start(), calls=%async_computation.4 | async-start | bytes 1310720 | tf_op jit(solution)/shard_map/all_gather | solution.py:105
  8.6 17.2 %all-to-all-start = ((s32[8,1,1]{2,1,0:T(1,128)}), s32[8,1,1]{2,1,0:T(1,128)S(1)}, u32[]{:S(2)}, u32[]{:S(2)}) async-start(s32[8,1,1]{2,1,0:T(1,128)} %copy.33), calls=%async_computation | async-start | bytes 8192 | tf_op jit(solution)/shard_map/all_to_all | solution.py:126
  15.9 0.7 copy-start.2
  16.7 0.7 copy-start.4
  22.6 0.7 copy-start.1
  25.8 12.4 %all-to-all-start.1 = ((s32[8,1,16]{2,1,0:T(1,128)}), s32[8,1,16]{2,1,0:T(1,128)S(1)}, u32[]{:S(2)}, u32[]{:S(2)}) async-start(s32[8,1,16]{2,1,0:T(1,128)} %param.12), calls=%async_computation.1 | async-start | bytes 8192 | tf_op jit(solution)/shard_map/all_to_all | solution.py:125
  39.5 7.0 %copy-start = (bf16[2,64,1024]{2,1,0:T(8,128)(2,1)S(1)}, bf16[2,64,1024]{2,1,0:T(8,128)(2,1)}, u32[]{:S(2)}) copy-start(bf16[2,64,1024]{2,1,0:T(8,128)(2,1)} %param.8) | copy-start | bytes 786436
  40.9 25.8 %collective-permute-start.6 = (bf16[1,16]{1,0:T(2,128)(2,1)S(1)}, bf16[1,16]{1,0:T(2,128)(2,1)S(1)}, u32[]{:S(2)}, u32[]{:S(2)}) collective-permute-start(bf16[1,16]{1,0:T(2,128)(2,1)S(1)} %get-tuple-element.192), channel_id=1, source_target_pairs={{0,28},{4,0},{8,4},{12,8},{16,12},{20,16},{24,20},{28,24},{1,29},{... | collective-permute-start | bytes 104 | tf_op jit(solution)/shard_map/ppermute | solution.py:36
  41.6 25.1 %collective-permute-start.5 = (bf16[1,16]{1,0:T(2,128)(2,1)S(1)}, bf16[1,16]{1,0:T(2,128)(2,1)S(1)}, u32[]{:S(2)}, u32[]{:S(2)}) collective-permute-start(bf16[1,16]{1,0:T(2,128)(2,1)S(1)} %get-tuple-element.193), channel_id=1, source_target_pairs={{0,24},{4,28},{8,0},{12,4},{16,8},{20,12},{24,16},{28,20},{1,25},{... | collective-permute-start | bytes 104 | tf_op jit(solution)/shard_map/ppermute | solution.py:36
  43.0 23.7 %collective-permute-start.4 = (bf16[1,16]{1,0:T(2,128)(2,1)S(1)}, bf16[1,16]{1,0:T(2,128)(2,1)S(1)}, u32[]{:S(2)}, u32[]{:S(2)}) collective-permute-start(bf16[1,16]{1,0:T(2,128)(2,1)S(1)} %get-tuple-element.194), channel_id=1, source_target_pairs={{0,20},{4,24},{8,28},{12,0},{16,4},{20,8},{24,12},{28,16},{1,21},{... | collective-permute-start | bytes 104 | tf_op jit(solution)/shard_map/ppermute | solution.py:36
  44.5 22.2 %collective-permute-start.3 = (bf16[1,16]{1,0:T(2,128)(2,1)S(1)}, bf16[1,16]{1,0:T(2,128)(2,1)S(1)}, u32[]{:S(2)}, u32[]{:S(2)}) collective-permute-start(bf16[1,16]{1,0:T(2,128)(2,1)S(1)} %get-tuple-element.195), channel_id=1, source_target_pairs={{0,16},{4,20},{8,24},{12,28},{16,0},{20,4},{24,8},{28,12},{1,17},{... | collective-permute-start | bytes 104 | tf_op jit(solution)/shard_map/ppermute | solution.py:36
  46.0 7.7 %collective-permute-start = (bf16[1,16]{1,0:T(2,128)(2,1)S(1)}, bf16[1,16]{1,0:T(2,128)(2,1)S(1)}, u32[]{:S(2)}, u32[]{:S(2)}) collective-permute-start(bf16[1,16]{1,0:T(2,128)(2,1)S(1)} %get-tuple-element.198), channel_id=1, source_target_pairs={{0,4},{4,8},{8,12},{12,16},{16,20},{20,24},{24,28},{28,0},{1,5},{5... | collective-permute-start | bytes 104 | tf_op jit(solution)/shard_map/ppermute | solution.py:36
  48.2 19.3 %all-to-all-start.2 = ((bf16[8,16,1024]{2,1,0:T(8,128)(2,1)}), bf16[8,16,1024]{2,1,0:T(8,128)(2,1)S(1)}, u32[]{:S(2)}, u32[]{:S(2)}) async-start(bf16[8,16,1024]{2,1,0:T(8,128)(2,1)} %broadcast_select_fusion), calls=%async_computation.2 | async-start | bytes 524288 | tf_op jit(solution)/shard_map/all_to_all | solution.py:132
  53.6 7.7 %collective-permute-start.1 = (bf16[1,16]{1,0:T(2,128)(2,1)S(1)}, bf16[1,16]{1,0:T(2,128)(2,1)S(1)}, u32[]{:S(2)}, u32[]{:S(2)}) collective-permute-start(bf16[1,16]{1,0:T(2,128)(2,1)S(1)} %get-tuple-element.197), channel_id=1, source_target_pairs={{0,8},{4,12},{8,16},{12,20},{16,24},{20,28},{24,0},{28,4},{1,9},{5... | collective-permute-start | bytes 104 | tf_op jit(solution)/shard_map/ppermute | solution.py:36
  61.3 5.4 %collective-permute-start.2 = (bf16[1,16]{1,0:T(2,128)(2,1)S(1)}, bf16[1,16]{1,0:T(2,128)(2,1)S(1)}, u32[]{:S(2)}, u32[]{:S(2)}) collective-permute-start(bf16[1,16]{1,0:T(2,128)(2,1)S(1)} %get-tuple-element.196), channel_id=1, source_target_pairs={{0,12},{4,16},{8,20},{12,24},{16,28},{20,0},{24,4},{28,8},{1,13},{... | collective-permute-start | bytes 104 | tf_op jit(solution)/shard_map/ppermute | solution.py:36
  96.3 10.1 %all-to-all-start.3 = ((f32[8,1,1]{2,1,0:T(1,128)}), f32[8,1,1]{2,1,0:T(1,128)S(1)}, u32[]{:S(2)}, u32[]{:S(2)}) async-start(f32[8,1,1]{2,1,0:T(1,128)} %copy.38), calls=%async_computation.3 | async-start | bytes 8192 | tf_op jit(solution)/shard_map/all_to_all | solution.py:142
Sparse Core Ops, SparseCore 0:
  9.5 19.4 all-gather.4
